TPU v7x, 32 devices: a whole 2x2x4 slice. The times are simulated.
32 devices in a mesh: dp: 8 (over y, x, core), mp: 4 (over z).
Axes of the slice: x: 2, y: 2, z: 4, core: 2. Of those that a mesh axis runs over, the one named last changes fastest.
Arguments:
- pre: bfloat16 [1024, 12288], P('dp', 'mp'), may hold values from -32 to 32
- weight: float32 [6144, 12288], P('dp', 'mp'), may hold values from -0.0546875 to 0.0546875
- target: bfloat16 [6144, 1024], P('dp'), may hold values from -100 to 100
Outputs:
- update: float32 [6144, 12288], P('dp', 'mp')
All inputs are finite; a program needn't handle non-finite values.
Results may differ from a plain program's by a relative error of at most 0.0003.
The roundings to bfloat16 on the way count: a program that leaves them out, or rounds other values in their place, can miss the bound.
Values may be sent and summed in bfloat16 or wider, within the bound.
A program may use at most 64 MiB of HBM per device.

v0:
```python
import jax
import jax.numpy as jnp
from jax import lax
from jax.sharding import PartitionSpec as P

radius = 0.005
epsilon = 1e-06


def on_device(pre, weight, target):
    hidden = jax.nn.gelu(pre.astype(jnp.float32), approximate=False).astype(jnp.bfloat16)
    everyone = lax.all_gather(hidden, "dp", axis=0, tiled=True)
    entries = weight.shape[0] * weight.shape[1] * lax.axis_size("dp") * lax.axis_size("mp")

    def residual_of(matrix):
        partial_out = lax.dot_general(
            matrix, everyone, (((1,), (1,)), ((), ())), preferred_element_type=jnp.float32
        )
        summed = lax.psum(partial_out, "mp")
        result = (summed - target.astype(jnp.float32)).astype(jnp.bfloat16)
        return result

    resid = residual_of(weight.astype(jnp.bfloat16))
    ascent = jnp.dot(resid, everyone, preferred_element_type=jnp.float32)
    ascent_ms = lax.psum(jnp.sum(ascent * ascent), ("dp", "mp")) / entries
    perturbed = (weight + radius * jnp.tanh(ascent / jnp.sqrt(ascent_ms + epsilon))).astype(
        jnp.bfloat16
    )
    resid_two = residual_of(perturbed)
    descent = jnp.dot(resid_two, everyone, preferred_element_type=jnp.float32)
    descent_ms = lax.psum(jnp.sum(descent * descent), ("dp", "mp")) / entries
    return descent / jnp.sqrt(descent_ms + epsilon)


def solution(mesh):
    return jax.shard_map(
        on_device,
        mesh=mesh,
        in_specs=(P("dp", "mp"), P("dp", "mp"), P("dp", None)),
        out_specs=P("dp", "mp"),
        check_vma=False,
    )
```

profile of v0, /device:TPU:0, one launch (start us, length us, event | category | flops | bytes accessed | tf_op | source)
XLA Modules:
  0.0 443.9 jit_solution(3158897468256516652)
XLA Ops:
  6.5 0.0 all-gather.2.cloned.1.call-start
  6.5 5.1 %fusion.9 = bf16[128,3072]{1,0:T(8,128)(2,1)} fusion(bf16[128,3072]{1,0:T(8,128)(2,1)} %param.3), kind=kLoop, calls=%fused_computation.16 | loop fusion | flops 25952256 | bytes 1572864 | tf_op jit(solution)/shard_map/convert_element_type | solution.py:11
  11.7 0.0 all-gather.2.cloned.1.call-update
  11.7 0.0 all-reduce.3.cloned.1.call-start
  11.8 48.3 %all-gather.2.cloned.1.call-done = bf16[1024,3072]{1,0:T(8,128)(2,1)} async-done(((bf16[128,3072]{1,0:T(8,128)(2,1)}), bf16[1024,3072]{1,0:T(8,128)(2,1)}) %all-gather.2.cloned.1.call-update) | async-done | bytes 6291472 | tf_op jit(solution)/shard_map/all_gather | solution.py:12
  60.1 11.1 %fusion.5 = f32[768,1024]{1,0:T(8,128)} fusion(bf16[1024,3072]{1,0:T(8,128)(2,1)} %all-gather.2.cloned.1.call-done, f32[768,3072]{1,0:T(8,128)} %param.4), kind=kOutput, calls=%fused_computation.14 | convolution fusion | flops 4834197504 | bytes 18874368 | tf_op jit(solution)/shard_map/dot_general | solution.py:16
  71.2 0.0 copy-start
  71.2 0.0 all-reduce.3.cloned.1.call-update
  71.2 0.0 all-reduce.5.cloned.1.call-start
  71.2 121.2 %all-reduce.3.cloned.1.call-done = f32[768,1024]{1,0:T(8,128)} async-done(((f32[768,1024]{1,0:T(8,128)}), f32[768,1024]{1,0:T(8,128)}) %all-reduce.3.cloned.1.call-update) | async-done | bytes 3145744 | tf_op jit(solution)/shard_map/psum | solution.py:19
  192.4 0.0 copy-done
  192.4 11.1 %multiply_reduce_fusion.1 = (f32[]{:T(128)}, f32[768,3072]{1,0:T(8,128)}) fusion(bf16[1024,3072]{1,0:T(8,128)(2,1)} %all-gather.2.cloned.1.call-done, f32[768,1024]{1,0:T(8,128)} %all-reduce.3.cloned.1.call-done, bf16[768,1024]{1,0:T(8,128)(2,1)S(1)} %copy-done), kind=kOutput, calls=%fused_computation.2 | convolution fusion | flops 4838916096 | bytes 20447236 | tf_op jit(solution)/shard_map/dot_general | solution.py:24
  203.5 39.6 %psum.29 = f32[]{:T(128)} all-reduce(f32[]{:T(128)} %get-tuple-element.5), channel_id=1, replica_groups=mesh['dp'=8,'mp'=4] {'dp','mp'}, use_global_device_ids=true, to_apply=%region_2.0 | all-reduce | flops 1 | bytes 8 | tf_op jit(solution)/shard_map/psum | solution.py:25
  243.7 12.1 %fusion.2 = f32[768,1024]{1,0:T(8,128)} fusion(bf16[1024,3072]{1,0:T(8,128)(2,1)} %all-gather.2.cloned.1.call-done, f32[768,3072]{1,0:T(8,128)} %param.4, f32[768,3072]{1,0:T(8,128)} %get-tuple-element.6, f32[]{:T(128)S(6)} %sqrt.6), kind=kOutput, calls=%fused_computation.6 | convolution fusion | flops 4841275392 | bytes 28311556 | tf_op jit(solution)/shard_map/dot_general | solution.py:16
  255.8 0.0 all-reduce.5.cloned.1.call-update
  255.9 121.2 %all-reduce.5.cloned.1.call-done = f32[768,1024]{1,0:T(8,128)} async-done(((f32[768,1024]{1,0:T(8,128)}), f32[768,1024]{1,0:T(8,128)}) %all-reduce.5.cloned.1.call-update) | async-done | bytes 3145744 | tf_op jit(solution)/shard_map/psum | solution.py:19
  377.1 11.1 %multiply_reduce_fusion = (f32[]{:T(128)}, f32[768,3072]{1,0:T(8,128)}) fusion(bf16[1024,3072]{1,0:T(8,128)(2,1)} %all-gather.2.cloned.1.call-done, f32[768,1024]{1,0:T(8,128)} %all-reduce.5.cloned.1.call-done, bf16[768,1024]{1,0:T(8,128)(2,1)S(1)} %copy-done), kind=kOutput, calls=%fused_computation | convolution fusion | flops 4838916096 | bytes 20447236 | tf_op jit(solution)/shard_map/dot_general | solution.py:30
  388.2 39.4 %psum.31 = f32[]{:T(128)} all-reduce(f32[]{:T(128)} %get-tuple-element.7), channel_id=1, replica_groups=mesh['dp'=8,'mp'=4] {'dp','mp'}, use_global_device_ids=true, to_apply=%region_5.0 | all-reduce | flops 1 | bytes 8 | tf_op jit(solution)/shard_map/psum | solution.py:31
  428.3 9.0 %broadcast_divide_fusion = f32[768,3072]{1,0:T(8,128)} fusion(f32[768,3072]{1,0:T(8,128)} %get-tuple-element.8, f32[]{:T(128)S(6)} %sqrt.7), kind=kLoop, calls=%fused_computation.3 | loop fusion | flops 2359296 | bytes 18874372 | tf_op jit(solution)/shard_map/div | solution.py:32
Async XLA Ops:
  6.5 53.5 %all-gather.2.cloned.1.call-start = ((), (), s32[]{:S(2)}) async-start(), calls=%async_computation | async-start | bytes 7077888 | tf_op jit(solution)/shard_map/all_gather | solution.py:12
  11.7 180.7 %all-reduce.3.cloned.1.call-start = ((), (), s32[]{:S(2)}) async-start(), calls=%async_computation.1 | async-start | bytes 6291456 | tf_op jit(solution)/shard_map/psum | solution.py:19
  71.2 121.3 %copy-start = (bf16[768,1024]{1,0:T(8,128)(2,1)S(1)}, bf16[768,1024]{1,0:T(8,128)(2,1)}, u32[]{:S(2)}) copy-start(bf16[768,1024]{1,0:T(8,128)(2,1)} %param.5) | copy-start | bytes 4718596
  71.2 305.9 %all-reduce.5.cloned.1.call-start = ((), (), s32[]{:S(2)}) async-start(), calls=%async_computation.2 | async-start | bytes 6291456 | tf_op jit(solution)/shard_map/psum | solution.py:19
Sparse Core Ops, SparseCore 0:
  11.8 48.2 all-gather.1
  71.3 121.0 all-reduce.2
  256.0 121.0 all-reduce.4
where the time goes:
time: 444 us
  waiting for transfers between devices  291 us (66%)
  blocking collectives  79 us (18%)
  matrix products  45.4 us (10%)
  between operations  14.5 us (3%)
  other arithmetic  14.2 us (3%)
    psum x2, waiting for transfers between devices, residual_of(): summed = lax.psum(partial_out, 'mp')  242 us
    all_gather x1, waiting for transfers between devices, on_device(): everyone = lax.all_gather(hidden, 'dp', axis=0, tiled=True)  48.3 us
    psum x1, blocking collectives, on_device(): ascent_ms = lax.psum(jnp.sum(ascent * ascent), ('dp', 'mp')) / entries  39.6 us
    psum x1, blocking collectives, on_device(): descent_ms = lax.psum(jnp.sum(descent * descent), ('dp', 'mp')) / entries  39.4 us
    dot_general x2, matrix products, residual_of(): lax.dot_general(matrix, everyone, (((1,), (1,)), ((), ())), preferred_ele...  23.2 us
    dot_general x1, matrix products, on_device(): ascent = jnp.dot(resid, everyone, preferred_element_type=jnp.float32)  11.1 us
    dot_general x1, matrix products, on_device(): descent = jnp.dot(resid_two, everyone, preferred_element_type=jnp.float32)  11.1 us
    div x1, other arithmetic, on_device(): return descent / jnp.sqrt(descent_ms + epsilon)  9.05 us
  transfers between devices with their start and end apart: 3, of which 3 were waited for; matrix products, arithmetic and copies ran while one was open for 0% of the time, Pallas kernels for 0%

commit v1 on v0

v1 whole, which is shorter than its diff:
```python
import functools

import jax
import jax.numpy as jnp
from jax import lax
from jax.experimental import pallas as pl
from jax.experimental.pallas import tpu as pltpu
from jax.sharding import PartitionSpec as P

radius = 0.005
epsilon = 1e-06
LAG = 1
MESH = pl.DeviceIdType.MESH


def on_device_plain(pre, weight, target):
    hidden = jax.nn.gelu(pre.astype(jnp.float32), approximate=False).astype(jnp.bfloat16)
    everyone = lax.all_gather(hidden, "dp", axis=0, tiled=True)
    entries = weight.shape[0] * weight.shape[1] * lax.axis_size("dp") * lax.axis_size("mp")

    def residual_of(matrix):
        partial_out = lax.dot_general(
            matrix, everyone, (((1,), (1,)), ((), ())), preferred_element_type=jnp.float32
        )
        summed = lax.psum(partial_out, "mp")
        return (summed - target.astype(jnp.float32)).astype(jnp.bfloat16)

    resid = residual_of(weight.astype(jnp.bfloat16))
    ascent = jnp.dot(resid, everyone, preferred_element_type=jnp.float32)
    ascent_ms = lax.psum(jnp.sum(ascent * ascent), ("dp", "mp")) / entries
    perturbed = (weight + radius * jnp.tanh(ascent / jnp.sqrt(ascent_ms + epsilon))).astype(
        jnp.bfloat16
    )
    resid_two = residual_of(perturbed)
    descent = jnp.dot(resid_two, everyone, preferred_element_type=jnp.float32)
    descent_ms = lax.psum(jnp.sum(descent * descent), ("dp", "mp")) / entries
    return descent / jnp.sqrt(descent_ms + epsilon)


def kernel(
    N, M, entries, C,
    hid_hbm, w_hbm, t_hbm, des_hbm, tot_ref,
    w, wl, h, a, tg, r1, r2, own1, own2, rcv1, rcv2, pbuf, ssq, sm, sd, dsum,
    ld, ags, agr, cs, cr, ss, sr, od,
):
    rows, ff = w.shape
    tokens = tg.shape[1]
    blk = tokens // N
    half = rows // 2
    dp = lax.axis_index("dp")
    z = lax.axis_index("mp")
    b0 = lax.rem(dp, 2)
    b1 = lax.rem(dp // 2, 2)
    b2 = dp // 4
    ds_ = 1 - 2 * b0
    dx = 2 * (1 - 2 * b1)
    dy = 4 * (1 - 2 * b2)
    sib = dp + ds_
    p = dp + (1 - b0) * dx + b0 * dy
    q = dp + b0 * dx + (1 - b0) * dy
    diag = dp + dx + dy
    sibp = q + ds_
    sibq = p + ds_
    sibd = diag + ds_

    def load(i, src, dst):
        return pltpu.make_async_copy(src, dst, ld.at[i])

    def tok(b, lo=0, n=blk):
        return pl.ds(pl.multiple_of(b * blk + lo, 16), n)

    load_h = load(0, hid_hbm, h.at[tok(dp), :])
    load_w = load(1, w_hbm, w)
    load_t = load(2, t_hbm, tg)
    load_h.start()
    load_w.start()
    load_t.start()

    barrier = pltpu.get_barrier_semaphore()
    for k in range(1, N):
        pl.semaphore_signal(barrier, inc=1, device_id=(lax.rem(dp + k, N), z), device_id_type=MESH)
    for k in range(1, M):
        pl.semaphore_signal(barrier, inc=1, device_id=(dp, lax.rem(z + k, M)), device_id_type=MESH)
    pl.semaphore_wait(barrier, N + M - 2)

    def gather(i, block, to, lo=0, n=blk):
        return pltpu.make_async_remote_copy(
            src_ref=h.at[tok(block, lo, n), :], dst_ref=h.at[tok(block, lo, n), :],
            send_sem=ags.at[i], recv_sem=agr.at[i],
            device_id=(to, z), device_id_type=MESH,
        )

    hb = blk // 2
    S, PP, Q, SP, SQ, RPQ, RQP, SD = range(8)
    sends = {
        S: gather(S, dp, sib), PP: gather(PP, dp, p), Q: gather(Q, dp, q),
        SP: gather(SP, p, sib), SQ: gather(SQ, q, sib),
        RPQ: gather(RPQ, p, q, 0, hb), RQP: gather(RQP, q, p, hb, hb),
        SD: gather(SD, diag, sib),
    }
    recvs = {
        S: gather(S, sib, sib), PP: gather(PP, p, p), Q: gather(Q, q, q),
        SP: gather(SP, sibp, sib), SQ: gather(SQ, sibq, sib),
        RPQ: gather(RPQ, diag, q, 0, hb), RQP: gather(RQP, diag, p, hb, hb),
        SD: gather(SD, sibd, sib),
    }
    load_h.wait()
    sends[PP].start()
    sends[S].start()
    load_w.wait()

    def cast(i, _):
        rs = pl.ds(pl.multiple_of(i * 64, 64), 64)
        wl[rs, :] = w[rs, :].astype(jnp.bfloat16)
        return 0

    lax.fori_loop(0, rows // 64, cast, 0)
    load_t.wait()

    order = [dp, sib, p, sibp, q, sibq, diag, sibd]

    def block_of(c):
        out = order[0] * 0
        for k in range(N):
            out = out + order[k] * (1 - jnp.minimum(jnp.abs(c - k), 1))
        return out

    UP, DOWN, RUP, RDOWN = range(4)

    def move(kind, c, src, dst, to):
        return pltpu.make_async_remote_copy(
            src_ref=src, dst_ref=dst, send_sem=cs.at[kind, c], recv_sem=cr.at[kind, c],
            device_id=(dp, to), device_id_type=MESH,
        )

    zu = lax.rem(z + 1, M)
    zd = lax.rem(z + M - 1, M)

    def chain(produce, own_at, rcv_at, res_at, tgt_of, on_up, on_down):
        def step(s, _):
            @pl.when(s < C)
            def _():
                produce(s)

            def reduce_one(kind, rkind, which, lag, is_head, is_tail, to, back):
                c = s - lag

                @pl.when((c >= 0) & (c < C))
                def _():
                    own = own_at(c, which)

                    @pl.when(jnp.logical_not(is_head))
                    def _():
                        move(kind, c, own, rcv_at(c, which), to).wait_recv()

                    @pl.when(jnp.logical_not(is_head | is_tail))
                    def _():
                        own[...] = own[...] + rcv_at(c, which)[...]

                    @pl.when(jnp.logical_not(is_tail))
                    def _():
                        move(kind, c, own, rcv_at(c, which), to).start()

                    @pl.when(is_tail)
                    def _():
                        total = own[...] + rcv_at(c, which)[...]
                        res_at(c, which)[...] = (
                            total - tgt_of(c, which)[...].astype(jnp.float32)
                        ).astype(jnp.bfloat16)
                        move(rkind, c, res_at(c, which), res_at(c, which), back).start()

            def back_one(rkind, which, lag, is_owner, is_last, to, done):
                c = s - lag

                @pl.when((c >= 0) & (c < C))
                def _():
                    @pl.when(jnp.logical_not(is_owner))
                    def _():
                        m = move(rkind, c, res_at(c, which), res_at(c, which), to)
                        m.wait_recv()

                        @pl.when(jnp.logical_not(is_last))
                        def _():
                            m.start()

                    if done is not None:
                        done(c)

            first, last = z == 0, z == M - 1
            reduce_one(UP, RUP, 0, LAG * z, first, last, zu, zd)
            reduce_one(DOWN, RDOWN, 1, LAG * (M - 1 - z), last, first, zd, zu)
            back_one(RUP, 0, LAG * (2 * (M - 1) - z), last, first, zd, on_up)
            back_one(RDOWN, 1, LAG * (M - 1 + z), first, last, zu, on_down)
            return 0

        lax.fori_loop(0, C + 2 * LAG * (M - 1), step, 0)

        def drain(c, _):
            @pl.when(z < M - 1)
            def _():
                move(UP, c, own_at(c, 0), rcv_at(c, 0), zu).wait_send()
                move(RDOWN, c, res_at(c, 1), res_at(c, 1), zu).wait_send()

            @pl.when(z > 0)
            def _():
                move(DOWN, c, own_at(c, 1), rcv_at(c, 1), zd).wait_send()
                move(RUP, c, res_at(c, 0), res_at(c, 0), zd).wait_send()

            return 0

        lax.fori_loop(0, C, drain, 0)

    def produce_one(s):
        @pl.when(s == 1)
        def _():
            recvs[S].wait_recv()

        @pl.when(s == 2)
        def _():
            recvs[PP].wait_recv()
            sends[SP].start()
            sends[Q].start()

        @pl.when(s == 3)
        def _():
            recvs[SP].wait_recv()

        @pl.when(s == 4)
        def _():
            recvs[Q].wait_recv()
            sends[RPQ].start()
            sends[RQP].start()
            sends[SQ].start()

        @pl.when(s == 5)
        def _():
            recvs[SQ].wait_recv()

        @pl.when(s == 6)
        def _():
            recvs[RPQ].wait_recv()
            recvs[RQP].wait_recv()
            sends[SD].start()

        @pl.when(s == 7)
        def _():
            recvs[SD].wait_recv()

        hb_ = h[tok(block_of(s)), :]
        own1[s] = lax.dot_general(
            wl[...], hb_, (((1,), (1,)), ((), ())), preferred_element_type=jnp.float32
        )

    def cols(c):
        return pl.ds(pl.multiple_of(block_of(c) * blk, blk), blk)

    def one(ref):
        return lambda c, which: ref.at[c, pl.ds(which * half, half), :]

    def colwise(ref):
        return lambda c, which: ref.at[pl.ds(which * half, half), cols(c)]

    chain(produce_one, one(own1), one(rcv1), colwise(r1), colwise(tg), None, None)
    for i in range(8):
        sends[i].wait_send()

    def total_squares(rnd):
        v = ssq[...]
        part = v[:, 0:128]
        for k in range(1, v.shape[1] // 128):
            part = part + v[:, 128 * k:128 * (k + 1)]

        def small(buf, lane, i, me, to):
            return pltpu.make_async_remote_copy(
                src_ref=buf.at[me], dst_ref=buf.at[me],
                send_sem=ss.at[rnd, lane, i], recv_sem=sr.at[rnd, lane, i],
                device_id=to, device_id_type=MESH,
            )

        mb = sm.at[rnd]
        db = sd.at[rnd]
        mb[z] = part
        up = [(dp, lax.rem(z + k, M)) for k in range(M)]
        dn = [lax.rem(z + M - k, M) for k in range(M)]
        for k in range(1, M):
            small(mb, 0, k, z, up[k]).start()
        for k in range(1, M):
            small(mb, 0, k, dn[k], up[k]).wait_recv()
        for k in range(1, M):
            small(mb, 0, k, z, up[k]).wait_send()
        got = mb[0]
        for k in range(1, M):
            got = got + mb[k]
        db[dp] = got
        upd = [(lax.rem(dp + k, N), z) for k in range(N)]
        dnd = [lax.rem(dp + N - k, N) for k in range(N)]
        for k in range(1, N):
            small(db, 1, k, dp, upd[k]).start()
        for k in range(1, N):
            small(db, 1, k, dnd[k], upd[k]).wait_recv()
        for k in range(1, N):
            small(db, 1, k, dp, upd[k]).wait_send()
        got = db[0]
        for k in range(1, N):
            got = got + db[k]
        return jnp.sum(jnp.sum(got, axis=0, keepdims=True), axis=1, keepdims=True)

    def squares(d):
        return (d * d).reshape(d.shape[0] // 8, 8, d.shape[1]).sum(axis=0)

    wide = ssq.shape[1]
    ssq[...] = jnp.zeros_like(ssq)

    def ascend(i, _):
        cs_ = pl.ds(pl.multiple_of(i * wide, wide), wide)
        d = jnp.dot(r1[...], h[:, cs_], preferred_element_type=jnp.float32)
        a[:, cs_] = d
        ssq[...] += squares(d)
        return 0

    lax.fori_loop(0, ff // wide, ascend, 0)
    scale = 1.0 / jnp.sqrt(total_squares(0) / entries + epsilon)
    ssq[...] = jnp.zeros_like(ssq)

    sub = half // C
    strip = tokens // 4

    def rws(c, which):
        return pl.ds(pl.multiple_of(which * half + c * sub, 16), sub)

    def produce_two(s):
        for which in range(2):
            rs = rws(s, which)
            pbuf[which * sub:(which + 1) * sub, :] = (
                w[rs, :] + radius * jnp.tanh(a[rs, :] * scale)
            ).astype(jnp.bfloat16)

        def part(i, _):
            ts = pl.ds(pl.multiple_of(i * strip, strip), strip)
            d = lax.dot_general(
                pbuf[...], h[ts, :], (((1,), (1,)), ((), ())), preferred_element_type=jnp.float32
            )
            own2[rws(s, 0), ts] = d[:sub]
            own2[rws(s, 1), ts] = d[sub:]
            return 0

        lax.fori_loop(0, tokens // strip, part, 0)

    def out_copy(c, which):
        return pltpu.make_async_copy(a.at[rws(c, which), :], des_hbm.at[rws(c, which), :], od.at[which, c])

    def descend(which):
        def run(c):
            def part(i, _):
                cs_ = pl.ds(pl.multiple_of(i * wide, wide), wide)
                d = jnp.dot(r2[rws(c, which), :], h[:, cs_], preferred_element_type=jnp.float32)
                a[rws(c, which), cs_] = d
                ssq[...] += squares(d)
                return 0

            lax.fori_loop(0, ff // wide, part, 0)
            out_copy(c, which).start()

        return run

    def rowwise(ref):
        return lambda c, which: ref.at[rws(c, which), :]

    chain(produce_two, rowwise(own2), rowwise(rcv2), rowwise(r2), rowwise(tg), descend(0), descend(1))
    tot_ref[...] = jnp.broadcast_to(total_squares(1), tot_ref.shape)

    def drain_out(c, _):
        out_copy(c, 0).wait()
        out_copy(c, 1).wait()
        return 0

    lax.fori_loop(0, C, drain_out, 0)


def on_device(N, M, pre, weight, target):
    hidden = jax.nn.gelu(pre.astype(jnp.float32), approximate=False).astype(jnp.bfloat16)
    rows, ff = weight.shape
    tokens = target.shape[1]
    entries = rows * ff * N * M
    C = N
    f32, bf16 = jnp.float32, jnp.bfloat16
    half = rows // 2
    blk = tokens // N
    any_ = pl.BlockSpec(memory_space=pl.ANY)
    descent, total = pl.pallas_call(
        functools.partial(kernel, N, M, float(entries), C),
        out_shape=(
            jax.ShapeDtypeStruct((rows, ff), f32),
            jax.ShapeDtypeStruct((8, 128), f32),
        ),
        in_specs=[any_, any_, any_],
        out_specs=(any_, pl.BlockSpec(memory_space=pltpu.VMEM)),
        scratch_shapes=[
            pltpu.VMEM((rows, ff), f32),
            pltpu.VMEM((rows, ff), bf16),
            pltpu.VMEM((tokens, ff), bf16),
            pltpu.VMEM((rows, ff), f32),
            pltpu.VMEM((rows, tokens), bf16),
            pltpu.VMEM((rows, tokens), bf16),
            pltpu.VMEM((rows, tokens), bf16),
            pltpu.VMEM((N, rows, blk), f32),
            pltpu.VMEM((rows, tokens), f32),
            pltpu.VMEM((N, rows, blk), f32),
            pltpu.VMEM((rows, tokens), f32),
            pltpu.VMEM((2 * half // C, ff), bf16),
            pltpu.VMEM((8, 512), f32),
            pltpu.VMEM((2, M, 8, 128), f32),
            pltpu.VMEM((2, N, 8, 128), f32),
            pltpu.VMEM((8, 128), f32),
            pltpu.SemaphoreType.DMA((3,)),
            pltpu.SemaphoreType.DMA((8,)),
            pltpu.SemaphoreType.DMA((8,)),
            pltpu.SemaphoreType.DMA((4, C)),
            pltpu.SemaphoreType.DMA((4, C)),
            pltpu.SemaphoreType.DMA((2, 2, max(N, M))),
            pltpu.SemaphoreType.DMA((2, 2, max(N, M))),
            pltpu.SemaphoreType.DMA((2, C)),
        ],
        compiler_params=pltpu.CompilerParams(
            collective_id=0, has_side_effects=True, vmem_limit_bytes=60 << 20
        ),
    )(hidden, weight, target)
    return descent / jnp.sqrt(total[0, 0] / entries + epsilon)


def solution(mesh):
    N, M = mesh.shape["dp"], mesh.shape["mp"]
    body = functools.partial(on_device, N, M) if (N, M) == (8, 4) else on_device_plain
    return jax.shard_map(
        body,
        mesh=mesh,
        in_specs=(P("dp", "mp"), P("dp", "mp"), P("dp", None)),
        out_specs=P("dp", "mp"),
        check_vma=False,
    )
```

time: 444 us -> 195 us (0.44)
  waiting for transfers between devices: 291 us -> 0 us
  Pallas kernels: 0 us -> 179 us
  blocking collectives: 79 us -> 0 us
  matrix products: 45.4 us -> 0 us
  between operations: 14.5 us -> 0.7 us
    psum x2 -> x0, waiting for transfers between devices: 242 us -> none  [residual_of(): summed = lax.psum(partial_out, 'mp')]
    pallas_call x0 -> x1, Pallas kernels: none -> 179 us  [on_device(): pl.pallas_call(functools.partial(kernel, N, M, float(entries), C), out_sh...]
    psum x2 -> x0, blocking collectives: 79 us -> none  [the longest x1 39.6 us: on_device(): ascent_ms = lax.psum(jnp.sum(ascent * ascent), ('dp', 'mp')) / entries]
    all_gather x1 -> x0, waiting for transfers between devices: 48.3 us -> none  [on_device(): everyone = lax.all_gather(hidden, 'dp', axis=0, tiled=True)]
    dot_general x4 -> x0, matrix products: 45.4 us -> none  [the longest x2 23.2 us: residual_of(): lax.dot_general(matrix, everyone, (((1,), (1,)), ((), ())), preferred_ele...]
  transfers between devices with their start and end apart: 3 -> 0, of which waited for: 3 -> 0; matrix products, arithmetic and copies ran while one was open for 0% -> 0% of each run, Pallas kernels for 0% -> 0%
where the time goes in v1:
time: 195 us
  Pallas kernels  179 us (92%)
  other arithmetic  14.2 us (7%)
    pallas_call x1, Pallas kernels, on_device(): pl.pallas_call(functools.partial(kernel, N, M, float(entries), C), out_sh...  179 us
    div x1, other arithmetic, on_device(): return descent / jnp.sqrt(total[0, 0] / entries + epsilon)  9.04 us
    convert_element_type x1, other arithmetic, on_device(): jax.nn.gelu(pre.astype(jnp.float32), approximate=False).astype(jnp.bfloat16)  5.14 us

profile of v1, /device:TPU:0, one launch (start us, length us, event | category | flops | bytes accessed | tf_op | source)
XLA Modules:
  0.0 195.1 jit_solution(10746458820294467214)
XLA Ops:
  0.0 5.1 %fusion.1.hid_hbm = bf16[128,3072]{1,0:T(8,128)(2,1)} fusion(bf16[128,3072]{1,0:T(8,128)(2,1)} %param.3), kind=kLoop, calls=%fused_computation.5 | loop fusion | flops 25952256 | bytes 1572864 | tf_op jit(solution)/shard_map/convert_element_type | solution.py:381
  5.1 179.1 %shard_map.37 = (f32[768,3072]{1,0:T(8,128)}, f32[8,128]{1,0:T(8,128)}) custom-call(bf16[128,3072]{1,0:T(8,128)(2,1)} %fusion.1.hid_hbm, f32[768,3072]{1,0:T(8,128)} %w_hbm.1, bf16[768,1024]{1,0:T(8,128)(2,1)} %t_hbm.1), custom_call_target="tpu_custom_call" | custom-call | tf_op jit(solution)/shard_map/pallas_call | solution.py:390
  184.2 1.2 slice.3
  186.1 9.0 %broadcast_divide_fusion = f32[768,3072]{1,0:T(8,128)} fusion(f32[768,3072]{1,0:T(8,128)} %get-tuple-element.7, f32[]{:T(128)} %bitcast), kind=kLoop, calls=%fused_computation | loop fusion | flops 2359296 | bytes 18874372 | tf_op jit(solution)/shard_map/div | solution.py:428

commit v2 on v1

--- a/solution.py
+++ b/solution.py
@@ -40,7 +40,7 @@
 def kernel(
     N, M, entries, C,
     hid_hbm, w_hbm, t_hbm, des_hbm, tot_ref,
-    w, wl, h, a, tg, r1, r2, own1, own2, rcv1, rcv2, pbuf, ssq, sm, sd, dsum,
+    w, wl, h, a, tg, r1, own1, rcv1, pbuf, ssq, sm, sd, dsum,
     ld, ags, agr, cs, cr, ss, sr, od,
 ):
     rows, ff = w.shape
@@ -247,20 +247,17 @@
             recvs[SD].wait_recv()
 
         hb_ = h[tok(block_of(s)), :]
-        own1[s] = lax.dot_general(
+        own1[:, cols(s)] = lax.dot_general(
             wl[...], hb_, (((1,), (1,)), ((), ())), preferred_element_type=jnp.float32
         )
 
     def cols(c):
         return pl.ds(pl.multiple_of(block_of(c) * blk, blk), blk)
 
-    def one(ref):
-        return lambda c, which: ref.at[c, pl.ds(which * half, half), :]
-
     def colwise(ref):
         return lambda c, which: ref.at[pl.ds(which * half, half), cols(c)]
 
-    chain(produce_one, one(own1), one(rcv1), colwise(r1), colwise(tg), None, None)
+    chain(produce_one, colwise(own1), colwise(rcv1), colwise(r1), colwise(tg), None, None)
     for i in range(8):
         sends[i].wait_send()
 
@@ -340,8 +337,8 @@
             d = lax.dot_general(
                 pbuf[...], h[ts, :], (((1,), (1,)), ((), ())), preferred_element_type=jnp.float32
             )
-            own2[rws(s, 0), ts] = d[:sub]
-            own2[rws(s, 1), ts] = d[sub:]
+            own1[rws(s, 0), ts] = d[:sub]
+            own1[rws(s, 1), ts] = d[sub:]
             return 0
 
         lax.fori_loop(0, tokens // strip, part, 0)
@@ -353,7 +350,7 @@
         def run(c):
             def part(i, _):
                 cs_ = pl.ds(pl.multiple_of(i * wide, wide), wide)
-                d = jnp.dot(r2[rws(c, which), :], h[:, cs_], preferred_element_type=jnp.float32)
+                d = jnp.dot(r1[rws(c, which), :], h[:, cs_], preferred_element_type=jnp.float32)
                 a[rws(c, which), cs_] = d
                 ssq[...] += squares(d)
                 return 0
@@ -366,7 +363,7 @@
     def rowwise(ref):
         return lambda c, which: ref.at[rws(c, which), :]
 
-    chain(produce_two, rowwise(own2), rowwise(rcv2), rowwise(r2), rowwise(tg), descend(0), descend(1))
+    chain(produce_two, rowwise(own1), rowwise(rcv1), rowwise(r1), rowwise(tg), descend(0), descend(1))
     tot_ref[...] = jnp.broadcast_to(total_squares(1), tot_ref.shape)
 
     def drain_out(c, _):
@@ -385,7 +382,6 @@
     C = N
     f32, bf16 = jnp.float32, jnp.bfloat16
     half = rows // 2
-    blk = tokens // N
     any_ = pl.BlockSpec(memory_space=pl.ANY)
     descent, total = pl.pallas_call(
         functools.partial(kernel, N, M, float(entries), C),
@@ -402,10 +398,7 @@
             pltpu.VMEM((rows, ff), f32),
             pltpu.VMEM((rows, tokens), bf16),
             pltpu.VMEM((rows, tokens), bf16),
-            pltpu.VMEM((rows, tokens), bf16),
-            pltpu.VMEM((N, rows, blk), f32),
             pltpu.VMEM((rows, tokens), f32),
-            pltpu.VMEM((N, rows, blk), f32),
             pltpu.VMEM((rows, tokens), f32),
             pltpu.VMEM((2 * half // C, ff), bf16),
             pltpu.VMEM((8, 512), f32),
@@ -422,10 +415,10 @@
             pltpu.SemaphoreType.DMA((2, C)),
         ],
         compiler_params=pltpu.CompilerParams(
-            collective_id=0, has_side_effects=True, vmem_limit_bytes=60 << 20
+            collective_id=0, has_side_effects=True, vmem_limit_bytes=41 << 20
         ),
     )(hidden, weight, target)
-    return descent / jnp.sqrt(total[0, 0] / entries + epsilon)
+    return descent * (1.0 / jnp.sqrt(total[0, 0] / entries + epsilon))
 
 
 def solution(mesh):

time: 195 us -> 191 us (0.979)
  other arithmetic: 14.2 us -> 9.89 us
    div x1 -> x0, other arithmetic: 9.04 us -> none  [on_device(): return descent / jnp.sqrt(total[0, 0] / entries + epsilon)]
    mul x0 -> x1, other arithmetic: none -> 5.36 us  [on_device(): return descent * (1.0 / jnp.sqrt(total[0, 0] / entries + epsilon))]
where the time goes in v2:
time: 191 us
  Pallas kernels  180 us (94%)
  other arithmetic  9.89 us (5%)
    pallas_call x1, Pallas kernels, on_device(): pl.pallas_call(functools.partial(kernel, N, M, float(entries), C), out_sh...  180 us
    mul x1, other arithmetic, on_device(): return descent * (1.0 / jnp.sqrt(total[0, 0] / entries + epsilon))  5.36 us
    convert_element_type x1, other arithmetic, on_device(): jax.nn.gelu(pre.astype(jnp.float32), approximate=False).astype(jnp.bfloat16)  4.53 us

profile of v2, /device:TPU:0, one launch (start us, length us, event | category | flops | bytes accessed | tf_op | source)
XLA Modules:
  0.0 190.8 jit_solution(12569418563006757386)
XLA Ops:
  0.0 0.0 copy-start
  0.0 4.5 %fusion.1.hid_hbm = bf16[128,3072]{1,0:T(8,128)(2,1)S(1)} fusion(bf16[128,3072]{1,0:T(8,128)(2,1)} %param.3), kind=kLoop, calls=%fused_computation.5 | loop fusion | flops 25952256 | bytes 1572864 | tf_op jit(solution)/shard_map/convert_element_type | solution.py:378
  4.5 0.0 copy-done
  4.5 179.7 %shard_map.37 = (f32[768,3072]{1,0:T(8,128)S(1)}, f32[8,128]{1,0:T(8,128)S(1)}) custom-call(bf16[128,3072]{1,0:T(8,128)(2,1)S(1)} %fusion.1.hid_hbm, f32[768,3072]{1,0:T(8,128)} %w_hbm.1, bf16[768,1024]{1,0:T(8,128)(2,1)S(1)} %copy-done), custom_call_target="tpu_custom_call" | custom-call | tf_op jit(solution)/shard_map/pallas_call | solution.py:386
  184.3 0.5 slice.3
  185.5 5.4 %broadcast_multiply_fusion = f32[768,3072]{1,0:T(8,128)} fusion(f32[768,3072]{1,0:T(8,128)S(1)} %get-tuple-element.7, f32[]{:T(128)} %bitcast), kind=kLoop, calls=%fused_computation | loop fusion | flops 2359296 | bytes 18874372 | tf_op jit(solution)/shard_map/mul | solution.py:421
Async XLA Ops:
  0.0 4.5 %copy-start = (bf16[768,1024]{1,0:T(8,128)(2,1)S(1)}, bf16[768,1024]{1,0:T(8,128)(2,1)}, u32[]{:S(2)}) copy-start(bf16[768,1024]{1,0:T(8,128)(2,1)} %t_hbm.1) | copy-start | bytes 4718596

commit v3 on v2

--- a/solution.py
+++ b/solution.py
@@ -136,7 +136,7 @@
     zu = lax.rem(z + 1, M)
     zd = lax.rem(z + M - 1, M)
 
-    def chain(produce, own_at, rcv_at, res_at, tgt_of, on_up, on_down):
+    def chain(produce, own_at, rcv_at, res_at, tgt_of, on_up, on_down, extra=None):
         def step(s, _):
             @pl.when(s < C)
             def _():
@@ -191,6 +191,8 @@
             reduce_one(DOWN, RDOWN, 1, LAG * (M - 1 - z), last, first, zd, zu)
             back_one(RUP, 0, LAG * (2 * (M - 1) - z), last, first, zd, on_up)
             back_one(RDOWN, 1, LAG * (M - 1 + z), first, last, zu, on_down)
+            if extra is not None:
+                extra(s)
             return 0
 
         lax.fori_loop(0, C + 2 * LAG * (M - 1), step, 0)
@@ -257,7 +259,28 @@
     def colwise(ref):
         return lambda c, which: ref.at[pl.ds(which * half, half), cols(c)]
 
-    chain(produce_one, colwise(own1), colwise(rcv1), colwise(r1), colwise(tg), None, None)
+    wide = ssq.shape[1]
+    early = N // 2
+    ready = early + 2 * LAG * (M - 1)
+    tiles = ff // wide
+
+    def ascent_of(lo, hi, cs_):
+        left = jnp.concatenate([r1[:, cols(c)] for c in range(lo, hi)], axis=1)
+        right = jnp.concatenate([h[tok(order[c]), cs_] for c in range(lo, hi)], axis=0)
+        return jnp.dot(left, right, preferred_element_type=jnp.float32)
+
+    def ascend_early(s):
+        @pl.when((s >= ready) & (2 * (s - ready) < tiles))
+        def _():
+            for k in range(2):
+                i = 2 * (s - ready) + k
+                cs_ = pl.ds(pl.multiple_of(i * wide, wide), wide)
+                a[:, cs_] = ascent_of(0, early, cs_)
+
+    chain(
+        produce_one, colwise(own1), colwise(rcv1), colwise(r1), colwise(tg), None, None,
+        ascend_early,
+    )
     for i in range(8):
         sends[i].wait_send()
 
@@ -305,12 +328,11 @@
     def squares(d):
         return (d * d).reshape(d.shape[0] // 8, 8, d.shape[1]).sum(axis=0)
 
-    wide = ssq.shape[1]
     ssq[...] = jnp.zeros_like(ssq)
 
     def ascend(i, _):
         cs_ = pl.ds(pl.multiple_of(i * wide, wide), wide)
-        d = jnp.dot(r1[...], h[:, cs_], preferred_element_type=jnp.float32)
+        d = a[:, cs_] + ascent_of(early, N, cs_)
         a[:, cs_] = d
         ssq[...] += squares(d)
         return 0

time: 191 us -> 189 us (0.990)
  Pallas kernels: 180 us -> 177 us
    pallas_call x1, Pallas kernels: 180 us -> 177 us  [on_device(): pl.pallas_call(functools.partial(kernel, N, M, float(entries), C), out_sh...]
where the time goes in v3:
time: 189 us; the launch traced here: 188 us
  Pallas kernels  177 us (94%)
  other arithmetic  9.89 us (5%)
    pallas_call x1, Pallas kernels, on_device(): pl.pallas_call(functools.partial(kernel, N, M, float(entries), C), out_sh...  177 us
    mul x1, other arithmetic, on_device(): return descent * (1.0 / jnp.sqrt(total[0, 0] / entries + epsilon))  5.36 us
    convert_element_type x1, other arithmetic, on_device(): jax.nn.gelu(pre.astype(jnp.float32), approximate=False).astype(jnp.bfloat16)  4.53 us

profile of v3, /device:TPU:0, one launch (start us, length us, event | category | flops | bytes accessed | tf_op | source)
XLA Modules:
  0.0 188.5 jit_solution(9443827239221359610)
XLA Ops:
  0.0 0.0 copy-start
  0.0 4.5 %fusion.1.hid_hbm = bf16[128,3072]{1,0:T(8,128)(2,1)S(1)} fusion(bf16[128,3072]{1,0:T(8,128)(2,1)} %param.3), kind=kLoop, calls=%fused_computation.5 | loop fusion | flops 25952256 | bytes 1572864 | tf_op jit(solution)/shard_map/convert_element_type | solution.py:400
  4.5 0.0 copy-done
  4.5 177.4 %shard_map.37 = (f32[768,3072]{1,0:T(8,128)S(1)}, f32[8,128]{1,0:T(8,128)S(1)}) custom-call(bf16[128,3072]{1,0:T(8,128)(2,1)S(1)} %fusion.1.hid_hbm, f32[768,3072]{1,0:T(8,128)} %w_hbm.1, bf16[768,1024]{1,0:T(8,128)(2,1)S(1)} %copy-done), custom_call_target="tpu_custom_call" | custom-call | tf_op jit(solution)/shard_map/pallas_call | solution.py:408
  181.9 0.5 slice.3
  183.1 5.4 %broadcast_multiply_fusion = f32[768,3072]{1,0:T(8,128)} fusion(f32[768,3072]{1,0:T(8,128)S(1)} %get-tuple-element.7, f32[]{:T(128)} %bitcast), kind=kLoop, calls=%fused_computation | loop fusion | flops 2359296 | bytes 18874372 | tf_op jit(solution)/shard_map/mul | solution.py:443
Async XLA Ops:
  0.0 4.5 %copy-start = (bf16[768,1024]{1,0:T(8,128)(2,1)S(1)}, bf16[768,1024]{1,0:T(8,128)(2,1)}, u32[]{:S(2)}) copy-start(bf16[768,1024]{1,0:T(8,128)(2,1)} %t_hbm.1) | copy-start | bytes 4718596
